TPU v7x, 512 devices: a whole 4x4x16 slice. The times are simulated.
512 devices in a mesh: role: 4 (over y), pairs: 128 (over x, z, core).
Axes of the slice: x: 4, y: 4, z: 16, core: 2. Of those that a mesh axis runs over, the one named last changes fastest.
Arguments:
- three_index: bfloat16 [256, 1024, 512], P('pairs'), may hold values from -6 to 6
- coeff: bfloat16 [512, 512, 256], P('pairs'), may hold values from -6 to 6
- amps: bfloat16 [512, 256, 256], P('pairs'), may hold values from -4 to 4
- eps_virt: float32 [512, 256], P('pairs'), may hold values from 0.3 to 3
- eps_occ: float32 [256], replicated, may hold values from -1.5 to -0.3
- nvirt: int32 [512], P('pairs'), may hold values from 64 to 256, as said below
- pair_occ: int32 [512, 2], P('pairs'), may hold values from 0 to 255, as said below
- partners: int32 [512, 8], P('pairs'), may hold values from 0 to 511, as said below
- coupling: float32 [512, 8], P('pairs'), may hold values from -1 to 1
- pair_owner: int32 [512], P('pairs'), may hold values from 1 to 3, as said below
Outputs:
- amps_out: bfloat16 [1024, 256, 256], P(('role', 'pairs'))
- dressed_out: bfloat16 [1024, 512, 256], P(('role', 'pairs'))
Inputs may be any that keep to these rules, and one draw needn't show every extreme that they name: `nvirt`: each block of 4 consecutive pairs has one pair with all 256 virtuals. `pair_occ`: for pair k in block c = k // 4, the first orbital is one of the 2 orbitals numbered from 2 * c, and the second is one of the 6 orbitals numbered cyclically from 2 * (c - 1) modulo 256. Pair k's partners are distinct pairs of its own block of 4 pairs and the blocks just before and after it, cyclically modulo 512. `pair_owner`: in each block of 4 consecutive pairs, each of the roles 1 to 3 holds one or two pairs and exactly one role holds two.
All inputs are finite; a program needn't handle non-finite values.
Results may differ from a plain program's by a relative error of at most 0.012.
Values may be sent and summed in bfloat16 or wider, within the bound.
A program may use at most 64 MiB of HBM per device.

v0:
```python
import math
import jax
import jax.numpy as jnp
from jax import lax
from jax.sharding import PartitionSpec as P

PARTNERS = 8
ITERS = 2
SLOTS = 2


def extended(cells, sides, width):
    for axis, dim in sides:
        count = lax.axis_size(axis)
        head = lax.slice_in_dim(cells, 0, width, axis=dim)
        tail = lax.slice_in_dim(cells, cells.shape[dim] - width, cells.shape[dim], axis=dim)
        cells = jnp.concatenate(
            [
                lax.ppermute(tail, axis, [(i, (i + 1) % count) for i in range(count)]),
                cells,
                lax.ppermute(head, axis, [((i + 1) % count, i) for i in range(count)]),
            ],
            axis=dim,
        )
    return cells


def from_root(value, axis, source):
    kept = jnp.where(lax.axis_index(axis) == source, value, 0).astype(value.dtype)
    return lax.psum(kept, axis)


def local(
    three_index, coeff, amps, eps_virt, eps_occ, nvirt, pair_occ, partners, coupling, pair_owner
):
    column_count = lax.axis_size("pairs")
    role_index = lax.axis_index("role")
    column = lax.axis_index("pairs")
    occ_block = three_index.shape[0]
    width_aux = three_index.shape[1]
    pair_block = coeff.shape[0]
    width_pao = coeff.shape[1]
    width_virt = coeff.shape[2]
    slot_count = SLOTS
    pao_scale = 1.0 / math.sqrt(width_pao)
    aux_scale = 1.0 / math.sqrt(width_aux)
    virt_scale = 1.0 / math.sqrt(width_virt)
    occ_local = jnp.mod(pair_occ - (column - 1) * occ_block, occ_block * column_count)
    partner_local = jnp.mod(partners - (column - 1) * pair_block, pair_block * column_count)
    positions = jnp.arange(pair_block, dtype=jnp.int32)
    same_owner = (pair_owner[:, None] == pair_owner[None, :]).astype(jnp.int32)
    earlier = (positions[None, :] < positions[:, None]).astype(jnp.int32)
    pair_ranks = jnp.sum(same_owner * earlier, axis=1)
    gathered_at = pair_owner * slot_count + pair_ranks
    owned_here = pair_owner == role_index
    slot_ids = jnp.arange(slot_count, dtype=jnp.int32)
    slot_hits = (owned_here[None, :] & (pair_ranks[None, :] == slot_ids[:, None])).astype(jnp.int32)
    slot_pair = jnp.sum(slot_hits * positions[None, :], axis=1)
    slot_valid = (jnp.sum(slot_hits, axis=1) > 0).astype(jnp.float32)
    virtuals = jnp.arange(width_virt, dtype=jnp.int32)
    blocks = extended(three_index, (("pairs", 0),), occ_block)

    def transform_rows(orbitals_all, first_ids, second_ids):

        def one_pair(packed):
            orbitals, first_at, second_at = packed
            first_half = (
                jnp.dot(blocks[first_at], orbitals, preferred_element_type=jnp.float32) * pao_scale
            ).astype(jnp.bfloat16)
            second_half = (
                jnp.dot(blocks[second_at], orbitals, preferred_element_type=jnp.float32) * pao_scale
            ).astype(jnp.bfloat16)
            return (
                jnp.einsum("qa,qb->ab", first_half, second_half, preferred_element_type=jnp.float32)
                * aux_scale
            )

        return lax.map(one_pair, (orbitals_all, first_ids, second_ids))

    def transform(orbitals_all):
        return transform_rows(orbitals_all, occ_local[:, 0], occ_local[:, 1])

    near_orbitals = extended(coeff, (("pairs", 0),), pair_block)

    def slot_intersections():

        def slot_one_slot(slot_at):
            pair_at = slot_pair[slot_at]
            partner_orb = near_orbitals[partner_local[pair_at]]
            return (
                jnp.einsum(
                    "mb,kmc->kbc", coeff[pair_at], partner_orb, preferred_element_type=jnp.float32
                )
                * (1.0 / width_pao)
            ).astype(jnp.bfloat16)

        return lax.map(slot_one_slot, slot_ids)

    intersections = lax.cond(
        role_index > 0,
        slot_intersections,
        lambda: jnp.zeros((slot_count, PARTNERS, width_virt, width_virt), jnp.bfloat16),
    )

    def refresh(slot_ints, amp_pairs, near_amps):

        def refresh_one_slot(slot_at):
            pair_at = slot_pair[slot_at]
            intersection = intersections[slot_at]
            partner_amp = near_amps[partner_local[pair_at]]
            middle = jnp.einsum(
                "kbc,kcd->kbd", intersection, partner_amp, preferred_element_type=jnp.float32
            ).astype(jnp.bfloat16)
            partner_terms = jnp.einsum(
                "kbd,ked->kbe", middle, intersection, preferred_element_type=jnp.float32
            )
            coupled = jnp.sum(coupling[pair_at][:, None, None] * partner_terms, axis=0)
            occ_shift = eps_occ[pair_occ[pair_at, 0]] + eps_occ[pair_occ[pair_at, 1]]
            energy = eps_virt[pair_at][:, None] + eps_virt[pair_at][None, :] - occ_shift
            own_amp = amp_pairs[pair_at].astype(jnp.float32)
            fresh_amp = own_amp - (
                slot_ints[slot_at].astype(jnp.float32) + energy * own_amp + coupled
            ) / (energy + 1.0)
            keep_rows = (virtuals < nvirt[pair_at]).astype(jnp.float32) * slot_valid[slot_at]
            fresh_amp = (fresh_amp * keep_rows[:, None] * keep_rows[None, :]).astype(jnp.bfloat16)
            dressed = (
                (
                    coeff[pair_at].astype(jnp.float32)
                    + jnp.dot(coeff[pair_at], fresh_amp, preferred_element_type=jnp.float32)
                    * virt_scale
                )
                * slot_valid[slot_at]
            ).astype(jnp.bfloat16)
            return (fresh_amp, dressed)

        return lax.map(refresh_one_slot, slot_ids)

    zero_amp = jnp.zeros((slot_count, width_virt, width_virt), jnp.bfloat16)
    zero_orb = jnp.zeros((slot_count, width_pao, width_virt), jnp.bfloat16)
    amp_pairs = amps
    orb_pairs = coeff
    slot_amps = zero_amp
    slot_orbs = jnp.take(coeff, slot_pair, axis=0)
    for iteration in range(ITERS):
        local_ints = lax.cond(
            role_index == 0,
            lambda: transform(orb_pairs).astype(jnp.bfloat16),
            lambda: jnp.zeros((pair_block, width_virt, width_virt), jnp.bfloat16),
        )
        pair_ints = from_root(local_ints, "role", 0)
        slot_ints = jnp.take(pair_ints, slot_pair, axis=0)
        near_amps = extended(amp_pairs, (("pairs", 0),), pair_block)
        slot_amps, slot_orbs = lax.cond(
            role_index > 0,
            lambda: refresh(slot_ints, amp_pairs, near_amps),
            lambda: (zero_amp, zero_orb),
        )
        if iteration + 1 < ITERS:
            every_amp, every_orb = (
                lax.all_gather(slot_amps, "role", axis=0, tiled=True),
                lax.all_gather(slot_orbs, "role", axis=0, tiled=True),
            )
            amp_pairs = jnp.take(every_amp, gathered_at, axis=0)
            orb_pairs = jnp.take(every_orb, gathered_at, axis=0)
    return (slot_amps, slot_orbs)


def solution(mesh):
    in_specs = (
        P("pairs", None, None),
        P("pairs", None, None),
        P("pairs", None, None),
        P("pairs", None),
        P(),
        P("pairs"),
        P("pairs", None),
        P("pairs", None),
        P("pairs", None),
        P("pairs"),
    )
    out_specs = (P(("role", "pairs"), None, None), P(("role", "pairs"), None, None))
    return jax.shard_map(local, mesh=mesh, in_specs=in_specs, out_specs=out_specs, check_vma=False)
```

profile of v0, /device:TPU:16, one launch (start us, length us, event | category | flops | bytes accessed | tf_op | source)
XLA Modules:
  0.0 408.3 jit_solution(528838157583865312)
XLA Ops:
  7.2 1.9 collective-permute-start
  9.1 13.0 %collective-permute-start.1 = (bf16[2,1024,512]{2,1,0:T(8,128)(2,1)}, bf16[2,1024,512]{2,1,0:T(8,128)(2,1)S(1)}, u32[]{:S(2)}, u32[]{:S(2)}) collective-permute-start(bf16[2,1024,512]{2,1,0:T(8,128)(2,1)} %param.32), channel_id=1, source_target_pairs={{1,0},{2,1},{3,2},{4,3},{5,4},{6,5},{7,6},{8,7},{9,8},{10,9},{11,1... | collective-permute-start | bytes 6291464 | tf_op jit(solution)/shard_map/ppermute | solution.py:21
  22.2 1.9 collective-permute-start.2
  24.1 7.0 %collective-permute-start.3 = (bf16[4,512,256]{2,1,0:T(8,128)(2,1)}, bf16[4,512,256]{2,1,0:T(8,128)(2,1)}, u32[]{:S(2)}, u32[]{:S(2)}) collective-permute-start(bf16[4,512,256]{2,1,0:T(8,128)(2,1)} %param.33), channel_id=1, source_target_pairs={{1,0},{2,1},{3,2},{4,3},{5,4},{6,5},{7,6},{8,7},{9,8},{10,9},{11,1... | collective-permute-start | bytes 3145736 | tf_op jit(solution)/shard_map/ppermute | solution.py:21
  31.1 1.9 collective-permute-start.4
  36.2 8.1 %collective-permute-done = bf16[2,1024,512]{2,1,0:T(8,128)(2,1)} collective-permute-done((bf16[2,1024,512]{2,1,0:T(8,128)(2,1)}, bf16[2,1024,512]{2,1,0:T(8,128)(2,1)}, u32[]{:S(2)}, u32[]{:S(2)}) %collective-permute-start) | collective-permute-done | bytes 2097184 | tf_op jit(solution)/shard_map/ppermute | solution.py:19
  44.3 1.9 collective-permute-start.5
  46.2 3.0 constant_dynamic-update-slice_fusion.4
  49.2 1.5 constant_dynamic-update-slice_fusion.3
  50.8 1.5 constant_dynamic-update-slice_fusion.2
  54.2 7.0 %collective-permute-done.4 = bf16[4,256,256]{2,1,0:T(8,128)(2,1)} collective-permute-done((bf16[4,256,256]{2,1,0:T(8,128)(2,1)}, bf16[4,256,256]{2,1,0:T(8,128)(2,1)}, u32[]{:S(2)}, u32[]{:S(2)}) %collective-permute-start.4) | collective-permute-done | bytes 524320 | tf_op jit(solution)/shard_map/ppermute | solution.py:19
  61.1 1.8 collective-permute-done.5
  62.9 2.5 pad_maximum_fusion.1
  65.4 2.0 pad_maximum_fusion
  67.5 20.9 %conditional.6 = (bf16[2,8,256,256]{2,3,1,0:T(8,128)(2,1)}) conditional(s32[]{:T(128)} %convert_element_type.100, () %tuple.66, (s32[2]{0:T(128)S(1)}, s32[2]{0:T(128)S(1)}, s32[4,8]{1,0:T(4,128)S(1)}, bf16[12,512,256]{2,1,0:T(8,128)(2,1)S(1)}, bf16[4,512,256]{2,1,0:T(8,128)(2,1)}) %tuple.67), branch_computations={%region_2.3_spmd, %region_3.6_spmd} | conditional | flops 537920512 | bytes 7607225 | solution.py:99
  67.6 20.9 %while.49 = (s32[]{:T(128)}, bf16[2,8,256,256]{2,3,1,0:T(8,128)(2,1)}, s32[2]{0:T(128)S(1)}, s32[2]{0:T(128)S(1)}, s32[4,8]{1,0:T(4,128)S(1)}, /*index=5*/bf16[1...) while((s32[]{:T(128)}, ...), condition=%wide.region_5.5_spmd, body=%wide.region_4.4_spmd.sunk | while | flops 537920512 | bytes 7607121 | solution.py:97
  72.6 2.0 gather_fusion.3
  74.7 3.3 fusion.176
  83.1 2.0 gather_fusion.3
  85.1 3.3 fusion.176
  88.4 54.3 %all-reduce.3.cloned.1.call-done = bf16[4,256,256]{2,1,0:T(8,128)(2,1)} async-done(((bf16[4,256,256]{2,1,0:T(8,128)(2,1)}), bf16[4,256,256]{2,1,0:T(8,128)(2,1)}) %all-reduce.3.cloned.1.call-update) | async-done | bytes 524304 | tf_op jit(solution)/shard_map/psum | solution.py:30
  142.7 1.6 gather_fusion.5
  144.4 42.6 %conditional.7 = (bf16[2,256,256]{2,1,0:T(8,128)(2,1)}, bf16[2,512,256]{2,1,0:T(8,128)(2,1)}) conditional(s32[]{:T(128)} %convert_element_type.100, () %tuple.63, (s32[2]{0:T(128)S(1)}, s32[2]{0:T(128)S(1)}, bf16[4,256,256]{2,1,0:T(8,128)(2,1)}, pred[2]{0:T(512)(128)(4,1)S(1)}, f32[4,256]{1,0:T(4,128)S(1)}, /*index=5*/s32[4,2]{0,1:T(2,128)S(1)}, ...), branch_computations={%region_12.14_spmd, %region_13.18_spmd} | conditional | flops 607127040 | bytes 12207015 | solution.py:153
  144.6 42.5 %while.52 = (s32[]{:T(128)}, bf16[2,256,256]{2,1,0:T(8,128)(2,1)}, bf16[2,512,256]{2,1,0:T(8,128)(2,1)}, s32[2]{0:T(128)S(1)}, s32[2]{0:T(128)S(1)}, /*index=5*/...) while((s32[]{:T(128)}, bf16[2,256,256]{2,1,0:T(8,128)(2,1)}, ...), condition=%wide.region_16.17_spmd, body=%wide.region_14.16_spmd.sunk | while | flops 606995968 | bytes 11420373 | solution.py:136
  149.5 2.0 gather_fusion.2
  151.6 2.4 multiply_reduce_fusion.5
  162.5 1.8 constant_dynamic-update-slice_fusion.8
  164.3 1.5 fusion.172
  170.8 2.0 gather_fusion.2
  172.8 2.4 multiply_reduce_fusion.5
  183.8 1.8 constant_dynamic-update-slice_fusion.8
  185.6 1.5 fusion.172
  187.9 31.6 %all-gather.3.cloned.1.call-done = bf16[8,256,256]{2,1,0:T(8,128)(2,1)} async-done(((bf16[2,256,256]{2,1,0:T(8,128)(2,1)}), bf16[8,256,256]{2,1,0:T(8,128)(2,1)}) %all-gather.3.cloned.1.call-update) | async-done | bytes 1048592 | tf_op jit(solution)/shard_map/all_gather | solution.py:160
  219.4 1.8 gather_fusion.4
  221.4 1.9 collective-permute-start.6
  223.3 7.0 %collective-permute-start.7 = (bf16[4,256,256]{2,1,0:T(8,128)(2,1)S(1)}, bf16[4,256,256]{2,1,0:T(8,128)(2,1)}, u32[]{:S(2)}, u32[]{:S(2)}) collective-permute-start(bf16[4,256,256]{2,1,0:T(8,128)(2,1)S(1)} %broadcast_select_fusion.3), channel_id=1, source_target_pairs={{1,0},{2,1},{3,2},{4,3},{5,4},{6,5},{7,6},{8,7},{9,8},{10,9},{11,1... | collective-permute-start | bytes 1572872 | tf_op jit(solution)/shard_map/ppermute | solution.py:21
  230.3 30.4 %all-gather.5.cloned.1.call-done = bf16[8,512,256]{2,1,0:T(8,128)(2,1)} async-done(((bf16[2,512,256]{2,1,0:T(8,128)(2,1)}), bf16[8,512,256]{2,1,0:T(8,128)(2,1)}) %all-gather.5.cloned.1.call-update) | async-done | bytes 2097168 | tf_op jit(solution)/shard_map/all_gather | solution.py:161
  263.2 1.4 pad_maximum_fusion.2
  264.6 93.4 %all-reduce.5.cloned.1.call-done = bf16[4,256,256]{2,1,0:T(8,128)(2,1)} async-done(((bf16[4,256,256]{2,1,0:T(8,128)(2,1)}), bf16[4,256,256]{2,1,0:T(8,128)(2,1)}) %all-reduce.5.cloned.1.call-update) | async-done | bytes 524304 | tf_op jit(solution)/shard_map/psum | solution.py:30
  358.0 1.6 gather_fusion.6
  359.6 42.2 %conditional.9 = (bf16[2,256,256]{2,1,0:T(8,128)(2,1)}, bf16[2,512,256]{2,1,0:T(8,128)(2,1)}) conditional(s32[]{:T(128)} %convert_element_type.100, () %tuple.62, (s32[2]{0:T(128)S(1)}, s32[2]{0:T(128)S(1)}, bf16[4,256,256]{2,1,0:T(8,128)(2,1)S(1)}, pred[2]{0:T(512)(128)(4,1)S(1)}, f32[4,256]{1,0:T(4,128)S(1)}, /*index=5*/s32[4,2]{0,1:T(2,128)S(1)}, ...), branch_computations={%region_22.24_spmd, %region_23.28_spmd} | conditional | flops 607127040 | bytes 8012683 | solution.py:153
  360.5 41.4 %while.53 = (s32[]{:T(128)}, bf16[2,256,256]{2,1,0:T(8,128)(2,1)}, bf16[2,512,256]{2,1,0:T(8,128)(2,1)}, s32[2]{0:T(128)S(1)}, s32[2]{0:T(128)S(1)}, /*index=5*/...) while((s32[]{:T(128)}, bf16[2,256,256]{2,1,0:T(8,128)(2,1)}, ...), condition=%wide.region_26.27_spmd, body=%wide.region_24.26_spmd.sunk | while | flops 606995968 | bytes 7226041 | solution.py:136
  366.2 2.4 multiply_reduce_fusion.4
  376.9 1.8 constant_dynamic-update-slice_fusion.7
  378.6 2.6 fusion.156
  386.9 2.3 multiply_reduce_fusion.4
  397.5 1.8 constant_dynamic-update-slice_fusion.7
  399.3 2.5 fusion.156
  (118 shorter events, 34.2 us)
Async XLA Ops:
  7.2 135.6 %all-reduce.3.cloned.1.call-start = ((), (), s32[]{:S(2)}) async-start(), calls=%async_computation | async-start | bytes 1048576 | tf_op jit(solution)/shard_map/psum | solution.py:30
  7.2 37.1 %collective-permute-start = (bf16[2,1024,512]{2,1,0:T(8,128)(2,1)}, bf16[2,1024,512]{2,1,0:T(8,128)(2,1)}, u32[]{:S(2)}, u32[]{:S(2)}) collective-permute-start(bf16[2,1024,512]{2,1,0:T(8,128)(2,1)} %param.32), channel_id=1, source_target_pairs={{0,1},{1,2},{2,3},{3,4},{4,5},{5,6},{6,7},{7,8},{8,9},{9,10},{10,1... | collective-permute-start | bytes 6291464 | tf_op jit(solution)/shard_map/ppermute | solution.py:19
  9.1 41.6 %collective-permute-start.1 = (bf16[2,1024,512]{2,1,0:T(8,128)(2,1)}, bf16[2,1024,512]{2,1,0:T(8,128)(2,1)S(1)}, u32[]{:S(2)}, u32[]{:S(2)}) collective-permute-start(bf16[2,1024,512]{2,1,0:T(8,128)(2,1)} %param.32), channel_id=1, source_target_pairs={{1,0},{2,1},{3,2},{4,3},{5,4},{6,5},{7,6},{8,7},{9,8},{10,9},{11,1... | collective-permute-start | bytes 6291464 | tf_op jit(solution)/shard_map/ppermute | solution.py:21
  22.2 43.2 %collective-permute-start.2 = (bf16[4,512,256]{2,1,0:T(8,128)(2,1)}, bf16[4,512,256]{2,1,0:T(8,128)(2,1)}, u32[]{:S(2)}, u32[]{:S(2)}) collective-permute-start(bf16[4,512,256]{2,1,0:T(8,128)(2,1)} %param.33), channel_id=1, source_target_pairs={{0,1},{1,2},{2,3},{3,4},{4,5},{5,6},{6,7},{7,8},{8,9},{9,10},{10,1... | collective-permute-start | bytes 3145736 | tf_op jit(solution)/shard_map/ppermute | solution.py:19
  24.1 41.3 %collective-permute-start.3 = (bf16[4,512,256]{2,1,0:T(8,128)(2,1)}, bf16[4,512,256]{2,1,0:T(8,128)(2,1)}, u32[]{:S(2)}, u32[]{:S(2)}) collective-permute-start(bf16[4,512,256]{2,1,0:T(8,128)(2,1)} %param.33), channel_id=1, source_target_pairs={{1,0},{2,1},{3,2},{4,3},{5,4},{6,5},{7,6},{8,7},{9,8},{10,9},{11,1... | collective-permute-start | bytes 3145736 | tf_op jit(solution)/shard_map/ppermute | solution.py:21
  31.1 30.0 %collective-permute-start.4 = (bf16[4,256,256]{2,1,0:T(8,128)(2,1)}, bf16[4,256,256]{2,1,0:T(8,128)(2,1)}, u32[]{:S(2)}, u32[]{:S(2)}) collective-permute-start(bf16[4,256,256]{2,1,0:T(8,128)(2,1)} %param.34), channel_id=1, source_target_pairs={{0,1},{1,2},{2,3},{3,4},{4,5},{5,6},{6,7},{7,8},{8,9},{9,10},{10,1... | collective-permute-start | bytes 1572872 | tf_op jit(solution)/shard_map/ppermute | solution.py:19
  36.2 13.1 %copy-start.1 = (bf16[2,1024,512]{2,1,0:T(8,128)(2,1)S(1)}, bf16[2,1024,512]{2,1,0:T(8,128)(2,1)}, u32[]{:S(2)}) copy-start(bf16[2,1024,512]{2,1,0:T(8,128)(2,1)} %param.32) | copy-start | bytes 6291460
  44.3 18.6 %collective-permute-start.5 = (bf16[4,256,256]{2,1,0:T(8,128)(2,1)}, bf16[4,256,256]{2,1,0:T(8,128)(2,1)}, u32[]{:S(2)}, u32[]{:S(2)}) collective-permute-start(bf16[4,256,256]{2,1,0:T(8,128)(2,1)} %param.34), channel_id=1, source_target_pairs={{1,0},{2,1},{3,2},{4,3},{5,4},{6,5},{7,6},{8,7},{9,8},{10,9},{11,1... | collective-permute-start | bytes 1572872 | tf_op jit(solution)/shard_map/ppermute | solution.py:21
  50.8 1.6 copy-start.2
  52.4 10.5 %copy-start = (bf16[4,256,256]{2,1,0:T(8,128)(2,1)S(1)}, bf16[4,256,256]{2,1,0:T(8,128)(2,1)}, u32[]{:S(2)}) copy-start(bf16[4,256,256]{2,1,0:T(8,128)(2,1)} %param.34) | copy-start | bytes 1572868
  54.1 165.4 %all-gather.3.cloned.1.call-start = ((), (), s32[]{:S(2)}) async-start(), calls=%async_computation.1 | async-start | bytes 1310720 | tf_op jit(solution)/shard_map/all_gather | solution.py:160
  67.5 76.9 %copy-start.5 = (s32[4,2]{0,1:T(2,128)S(1)}, s32[4,2]{0,1:T(2,128)}, u32[]{:S(2)}) copy-start(s32[4,2]{0,1:T(2,128)} %param.38) | copy-start | bytes 100
  67.5 76.9 %copy-start.6 = (f32[256]{0:T(256)S(1)}, f32[256]{0:T(256)}, u32[]{:S(2)}) copy-start(f32[256]{0:T(256)} %param.36) | copy-start | bytes 3076
  67.5 76.9 %copy-start.7 = (f32[4,256]{1,0:T(4,128)S(1)}, f32[4,256]{1,0:T(4,128)}, u32[]{:S(2)}) copy-start(f32[4,256]{1,0:T(4,128)} %param.35) | copy-start | bytes 12292
  67.5 76.9 %copy-start.8 = (f32[4,8]{1,0:T(4,128)S(1)}, f32[4,8]{1,0:T(4,128)}, u32[]{:S(2)}) copy-start(f32[4,8]{1,0:T(4,128)} %param.40) | copy-start | bytes 388
  67.5 76.9 %copy-start.9 = (s32[4]{0:T(128)S(1)}, s32[4]{0:T(128)}, u32[]{:S(2)}) copy-start(s32[4]{0:T(128)} %param.37) | copy-start | bytes 52
  151.6 12.8 %copy-start.3 = (bf16[4,512,256]{2,1,0:T(8,128)(2,1)S(1)}, bf16[4,512,256]{2,1,0:T(8,128)(2,1)}, u32[]{:S(2)}) copy-start(bf16[4,512,256]{2,1,0:T(8,128)(2,1)} %get-tuple-element.1188) | copy-start | bytes 3145732 | tf_op jit(solution)/shard_map/cond/branch_1_fun/while
  172.8 12.8 %copy-start.3 = (bf16[4,512,256]{2,1,0:T(8,128)(2,1)S(1)}, bf16[4,512,256]{2,1,0:T(8,128)(2,1)}, u32[]{:S(2)}) copy-start(bf16[4,512,256]{2,1,0:T(8,128)(2,1)} %get-tuple-element.1188) | copy-start | bytes 3145732 | tf_op jit(solution)/shard_map/cond/branch_1_fun/while
  187.1 73.6 %all-gather.5.cloned.1.call-start = ((), (), s32[]{:S(2)}) async-start(), calls=%async_computation.2 | async-start | bytes 2621440 | tf_op jit(solution)/shard_map/all_gather | solution.py:161
  187.8 170.2 %all-reduce.5.cloned.1.call-start = ((), (), s32[]{:S(2)}) async-start(), calls=%async_computation.3 | async-start | bytes 1048576 | tf_op jit(solution)/shard_map/psum | solution.py:30
  221.4 41.0 %collective-permute-start.6 = (bf16[4,256,256]{2,1,0:T(8,128)(2,1)S(1)}, bf16[4,256,256]{2,1,0:T(8,128)(2,1)S(1)}, u32[]{:S(2)}, u32[]{:S(2)}) collective-permute-start(bf16[4,256,256]{2,1,0:T(8,128)(2,1)S(1)} %broadcast_select_fusion.3), channel_id=1, source_target_pairs={{0,1},{1,2},{2,3},{3,4},{4,5},{5,6},{6,7},{7,8},{8,9},{9,10},{10,1... | collective-permute-start | bytes 1572872 | tf_op jit(solution)/shard_map/ppermute | solution.py:19
  223.3 39.9 %collective-permute-start.7 = (bf16[4,256,256]{2,1,0:T(8,128)(2,1)S(1)}, bf16[4,256,256]{2,1,0:T(8,128)(2,1)}, u32[]{:S(2)}, u32[]{:S(2)}) collective-permute-start(bf16[4,256,256]{2,1,0:T(8,128)(2,1)S(1)} %broadcast_select_fusion.3), channel_id=1, source_target_pairs={{1,0},{2,1},{3,2},{4,3},{5,4},{6,5},{7,6},{8,7},{9,8},{10,9},{11,1... | collective-permute-start | bytes 1572872 | tf_op jit(solution)/shard_map/ppermute | solution.py:21
  262.4 0.8 copy-start.4
Sparse Core Ops, SparseCore 0:
  54.2 88.4 all-reduce.2
  187.2 32.1 all-gather.2
  222.1 38.5 all-gather.4
  262.9 95.0 all-reduce.4
where the time goes:
time: 410 us; the launch traced here: 408 us
  waiting for transfers between devices  227 us (55%)
  loops' own time  42 us (10%)
  local copies, waits for them, and re-layouts  40.2 us (10%)
  starting transfers between devices  36.7 us (9%)
  matrix products  24.3 us (6%)
  other arithmetic  23.8 us (6%)
  between operations  14.1 us (3%)
    psum x2, waiting for transfers between devices, from_root(): return lax.psum(kept, axis)  148 us
    another operation x2, loops' own time, refresh(): return lax.map(refresh_one_slot, slot_ids)  34.3 us
    all_gather x1, waiting for transfers between devices, local(): lax.all_gather(slot_amps, 'role', axis=0, tiled=True)  31.6 us
    all_gather x1, waiting for transfers between devices, local(): lax.all_gather(slot_orbs, 'role', axis=0, tiled=True)  30.4 us
    ppermute x4, starting transfers between devices, extended(): lax.ppermute(head, axis, [((i + 1) % count, i) for i in range(count)])  28.9 us
    ppermute x4, waiting for transfers between devices, extended(): lax.ppermute(tail, axis, [(i, (i + 1) % count) for i in range(count)])  15.1 us
    dot_general x4, matrix products, refresh_one_slot(): jnp.einsum('kbd,ked->kbe', middle, intersection, preferred_element_type=j...  9.55 us
  transfers between devices with their start and end apart: 12, of which 7 were waited for; matrix products, arithmetic and copies ran while one was open for 8% of the time, Pallas kernels for 0%

commit v1 on v0

--- a/solution.py
+++ b/solution.py
@@ -7,6 +7,12 @@
 PARTNERS = 8
 ITERS = 2
 SLOTS = 2
+
+
+def summed_here(x, name):
+    terms = lax.all_gather(x, name, axis=0, tiled=False)
+    result = terms.sum(axis=0)
+    return result
 
 
 def extended(cells, sides, width):
@@ -27,7 +33,7 @@
 
 def from_root(value, axis, source):
     kept = jnp.where(lax.axis_index(axis) == source, value, 0).astype(value.dtype)
-    return lax.psum(kept, axis)
+    return summed_here(kept, axis)
 
 
 def local(

time: 410 us -> 339 us (0.83)
  the two profiles are of different devices: /device:TPU:16 before, /device:TPU:8 now
where the time goes in v1:
time: 339 us; the launch traced here: 337 us
  waiting for transfers between devices  152 us (45%)
  loops' own time  42.1 us (12%)
  starting transfers between devices  41.8 us (12%)
  local copies, waits for them, and re-layouts  36.3 us (11%)
  matrix products  26.5 us (8%)
  other arithmetic  24.7 us (7%)
  between operations  14.1 us (4%)
    all_gather x2, waiting for transfers between devices, summed_here(): terms = lax.all_gather(x, name, axis=0, tiled=False)  43.6 us
    all_gather x1, waiting for transfers between devices, local(): lax.all_gather(slot_orbs, 'role', axis=0, tiled=True)  37.9 us
    another operation x2, loops' own time, refresh(): return lax.map(refresh_one_slot, slot_ids)  35.4 us
    ppermute x4, starting transfers between devices, extended(): lax.ppermute(head, axis, [((i + 1) % count, i) for i in range(count)])  33.9 us
    ppermute x4, waiting for transfers between devices, extended(): lax.ppermute(tail, axis, [(i, (i + 1) % count) for i in range(count)])  33.1 us
    all_gather x1, waiting for transfers between devices, local(): lax.all_gather(slot_amps, 'role', axis=0, tiled=True)  32.7 us
    dot_general x4, matrix products, refresh_one_slot(): jnp.dot(coeff[pair_at], fresh_amp, preferred_element_type=jnp.float32)  10.3 us
    dot_general x4, matrix products, refresh_one_slot(): jnp.einsum('kbd,ked->kbe', middle, intersection, preferred_element_type=j...  9.36 us
  transfers between devices with their start and end apart: 12, of which 9 were waited for; matrix products, arithmetic and copies ran while one was open for 8% of the time, Pallas kernels for 0%

profile of v1, /device:TPU:8, one launch (start us, length us, event | category | flops | bytes accessed | tf_op | source)
XLA Modules:
  0.0 337.1 jit_solution(7923496088769236142)
XLA Ops:
  7.2 1.9 collective-permute-start
  9.1 13.0 %collective-permute-start.1 = (bf16[2,1024,512]{2,1,0:T(8,128)(2,1)}, bf16[2,1024,512]{2,1,0:T(8,128)(2,1)S(1)}, u32[]{:S(2)}, u32[]{:S(2)}) collective-permute-start(bf16[2,1024,512]{2,1,0:T(8,128)(2,1)} %param.32), channel_id=1, source_target_pairs={{1,0},{2,1},{3,2},{4,3},{5,4},{6,5},{7,6},{8,7},{9,8},{10,9},{11,1... | collective-permute-start | bytes 6291464 | tf_op jit(solution)/shard_map/ppermute | solution.py:27
  22.9 21.4 %collective-permute-done = bf16[2,1024,512]{2,1,0:T(8,128)(2,1)} collective-permute-done((bf16[2,1024,512]{2,1,0:T(8,128)(2,1)}, bf16[2,1024,512]{2,1,0:T(8,128)(2,1)}, u32[]{:S(2)}, u32[]{:S(2)}) %collective-permute-start) | collective-permute-done | bytes 2097184 | tf_op jit(solution)/shard_map/ppermute | solution.py:25
  44.3 3.1 constant_dynamic-update-slice_fusion.4
  47.3 1.5 constant_dynamic-update-slice_fusion.3
  48.8 1.5 constant_dynamic-update-slice_fusion.2
  52.2 1.9 collective-permute-start.2
  54.1 7.0 %collective-permute-start.3 = (bf16[4,512,256]{2,1,0:T(8,128)(2,1)S(1)}, bf16[4,512,256]{2,1,0:T(8,128)(2,1)}, u32[]{:S(2)}, u32[]{:S(2)}) collective-permute-start(bf16[4,512,256]{2,1,0:T(8,128)(2,1)S(1)} %copy-done.3), channel_id=1, source_target_pairs={{1,0},{2,1},{3,2},{4,3},{5,4},{6,5},{7,6},{8,7},{9,8},{10,9},{11,1... | collective-permute-start | bytes 3145736 | tf_op jit(solution)/shard_map/ppermute | solution.py:27
  61.1 1.9 collective-permute-start.4
  63.0 7.0 %collective-permute-start.5 = (bf16[4,256,256]{2,1,0:T(8,128)(2,1)S(1)}, bf16[4,256,256]{2,1,0:T(8,128)(2,1)}, u32[]{:S(2)}, u32[]{:S(2)}) collective-permute-start(bf16[4,256,256]{2,1,0:T(8,128)(2,1)S(1)} %copy-done.1), channel_id=1, source_target_pairs={{1,0},{2,1},{3,2},{4,3},{5,4},{6,5},{7,6},{8,7},{9,8},{10,9},{11,1... | collective-permute-start | bytes 1572872 | tf_op jit(solution)/shard_map/ppermute | solution.py:27
  70.4 6.8 %collective-permute-done.4 = bf16[4,256,256]{2,1,0:T(8,128)(2,1)S(1)} collective-permute-done((bf16[4,256,256]{2,1,0:T(8,128)(2,1)S(1)}, bf16[4,256,256]{2,1,0:T(8,128)(2,1)S(1)}, u32[]{:S(2)}, u32[]{:S(2)}) %collective-permute-start.4) | collective-permute-done | bytes 524320 | tf_op jit(solution)/shard_map/ppermute | solution.py:25
  77.2 1.8 collective-permute-done.5
  79.0 2.4 pad_maximum_fusion.1
  82.3 2.0 pad_maximum_fusion
  84.4 19.9 %conditional.6 = (bf16[2,8,256,256]{2,3,1,0:T(8,128)(2,1)}) conditional(s32[]{:T(128)} %convert_element_type.104, () %tuple.66, (s32[2]{0:T(128)S(1)}, s32[2]{0:T(128)S(1)}, s32[4,8]{1,0:T(4,128)S(1)}, bf16[12,512,256]{2,1,0:T(8,128)(2,1)S(1)}, bf16[4,512,256]{2,1,0:T(8,128)(2,1)}) %tuple.67), branch_computations={%region_2.3_spmd, %region_3.6_spmd} | conditional | flops 537920512 | bytes 7607225 | solution.py:105
  84.4 19.9 %while.49 = (s32[]{:T(128)}, bf16[2,8,256,256]{2,3,1,0:T(8,128)(2,1)}, s32[2]{0:T(128)S(1)}, s32[2]{0:T(128)S(1)}, s32[4,8]{1,0:T(4,128)S(1)}, /*index=5*/bf16[1...) while((s32[]{:T(128)}, ...), condition=%wide.region_5.5_spmd, body=%wide.region_4.4_spmd.sunk | while | flops 537920512 | bytes 7607121 | solution.py:103
  88.9 2.1 gather_fusion.3
  91.0 3.3 fusion.176
  98.7 2.1 gather_fusion.3
  100.8 3.5 %fusion.176 = bf16[2,8,256,256]{2,3,1,0:T(8,128)(2,1)} fusion(bf16[2,8,256,256]{2,3,1,0:T(8,128)(2,1)} %get-tuple-element.1206, s32[]{:T(128)} %get-tuple-element.1205, bf16[8,512,256]{2,1,0:T(8,128)(2,1)} %gather_fusion.3, bf16[4,512,256]{2,1,0:T(8,128)(2,1)} %get-tuple-element.1222, s32[]{:T(128)S(6)} %select_n.217), kind=kOutput, calls=%fused_computation.51.clone.1 | convolution fusion | flops 537919488 | bytes 3408388 | tf_op jit(solution)/shard_map/cond/branch_1_fun/while/body/eval_jaxpr/mb,kmc->kbc/dot_general | solution.py:97
  104.4 16.1 %all-gather.11.cloned.1.call-done = bf16[16,256,256]{2,1,0:T(8,128)(2,1)} async-done(((bf16[4,256,256]{2,1,0:T(8,128)(2,1)}), bf16[16,256,256]{2,1,0:T(8,128)(2,1)}) %all-gather.11.cloned.1.call-update) | async-done | bytes 2097168 | tf_op jit(solution)/shard_map/all_gather | solution.py:13
  120.4 2.0 reduce_sum.75
  123.1 42.9 %conditional.7 = (bf16[2,256,256]{2,1,0:T(8,128)(2,1)}, bf16[2,512,256]{2,1,0:T(8,128)(2,1)}) conditional(s32[]{:T(128)} %convert_element_type.104, () %tuple.63, (s32[2]{0:T(128)S(1)}, s32[2]{0:T(128)S(1)}, bf16[4,256,256]{2,1,0:T(8,128)(2,1)}, pred[2]{0:T(512)(128)(4,1)S(1)}, f32[4,256]{1,0:T(4,128)S(1)}, /*index=5*/s32[4,2]{0,1:T(2,128)S(1)}, ...), branch_computations={%region_12.14_spmd, %region_13.18_spmd} | conditional | flops 607127040 | bytes 8012683 | solution.py:159
  123.2 42.8 %while.52 = (s32[]{:T(128)}, bf16[2,256,256]{2,1,0:T(8,128)(2,1)}, bf16[2,512,256]{2,1,0:T(8,128)(2,1)}, s32[2]{0:T(128)S(1)}, s32[2]{0:T(128)S(1)}, /*index=5*/...) while((s32[]{:T(128)}, bf16[2,256,256]{2,1,0:T(8,128)(2,1)}, ...), condition=%wide.region_16.17_spmd, body=%wide.region_14.16_spmd.sunk | while | flops 606995968 | bytes 7226041 | solution.py:142
  128.9 2.3 multiply_reduce_fusion.5
  138.9 1.3 compare_select_fusion.13
  140.2 1.8 constant_dynamic-update-slice_fusion.8
  142.0 2.6 fusion.172
  150.3 2.4 multiply_reduce_fusion.5
  161.6 1.8 constant_dynamic-update-slice_fusion.8
  163.4 2.6 fusion.172
  166.8 37.9 %all-gather.9.cloned.1.call-done = bf16[8,512,256]{2,1,0:T(8,128)(2,1)} async-done(((bf16[2,512,256]{2,1,0:T(8,128)(2,1)}), bf16[8,512,256]{2,1,0:T(8,128)(2,1)}) %all-gather.9.cloned.1.call-update) | async-done | bytes 2097168 | tf_op jit(solution)/shard_map/all_gather | solution.py:167
  206.4 32.7 %all-gather.7.cloned.1.call-done = bf16[8,256,256]{2,1,0:T(8,128)(2,1)} async-done(((bf16[2,256,256]{2,1,0:T(8,128)(2,1)}), bf16[8,256,256]{2,1,0:T(8,128)(2,1)}) %all-gather.7.cloned.1.call-update) | async-done | bytes 1048592 | tf_op jit(solution)/shard_map/all_gather | solution.py:166
  239.1 1.8 gather_fusion.4
  241.1 1.9 collective-permute-start.6
  243.0 7.0 %collective-permute-start.7 = (bf16[4,256,256]{2,1,0:T(8,128)(2,1)S(1)}, bf16[4,256,256]{2,1,0:T(8,128)(2,1)S(1)}, u32[]{:S(2)}, u32[]{:S(2)}) collective-permute-start(bf16[4,256,256]{2,1,0:T(8,128)(2,1)S(1)} %broadcast_select_fusion.3), channel_id=1, source_target_pairs={{1,0},{2,1},{3,2},{4,3},{5,4},{6,5},{7,6},{8,7},{9,8},{10,9},{11,1... | collective-permute-start | bytes 1572872 | tf_op jit(solution)/shard_map/ppermute | solution.py:27
  250.0 4.9 %collective-permute-done.6 = bf16[4,256,256]{2,1,0:T(8,128)(2,1)S(1)} collective-permute-done((bf16[4,256,256]{2,1,0:T(8,128)(2,1)S(1)}, bf16[4,256,256]{2,1,0:T(8,128)(2,1)S(1)}, u32[]{:S(2)}, u32[]{:S(2)}) %collective-permute-start.6) | collective-permute-done | bytes 524320 | tf_op jit(solution)/shard_map/ppermute | solution.py:25
  254.9 1.8 collective-permute-done.7
  256.8 27.6 %all-gather.13.cloned.1.call-done = bf16[16,256,256]{2,1,0:T(8,128)(2,1)} async-done(((bf16[4,256,256]{2,1,0:T(8,128)(2,1)}), bf16[16,256,256]{2,1,0:T(8,128)(2,1)}) %all-gather.13.cloned.1.call-update) | async-done | bytes 2097168 | tf_op jit(solution)/shard_map/all_gather | solution.py:13
  284.4 2.0 reduce_sum.77
  286.9 43.6 %conditional.9 = (bf16[2,256,256]{2,1,0:T(8,128)(2,1)}, bf16[2,512,256]{2,1,0:T(8,128)(2,1)}) conditional(s32[]{:T(128)} %convert_element_type.104, () %tuple.62, (s32[2]{0:T(128)S(1)}, s32[2]{0:T(128)S(1)}, bf16[4,256,256]{2,1,0:T(8,128)(2,1)S(1)}, pred[2]{0:T(512)(128)(4,1)S(1)}, f32[4,256]{1,0:T(4,128)S(1)}, /*index=5*/s32[4,2]{0,1:T(2,128)S(1)}, ...), branch_computations={%region_22.24_spmd, %region_23.28_spmd} | conditional | flops 607127040 | bytes 8012683 | solution.py:159
  287.8 42.8 %while.53 = (s32[]{:T(128)}, bf16[2,256,256]{2,1,0:T(8,128)(2,1)}, bf16[2,512,256]{2,1,0:T(8,128)(2,1)}, s32[2]{0:T(128)S(1)}, s32[2]{0:T(128)S(1)}, /*index=5*/...) while((s32[]{:T(128)}, bf16[2,256,256]{2,1,0:T(8,128)(2,1)}, ...), condition=%wide.region_26.27_spmd, body=%wide.region_24.26_spmd.sunk | while | flops 606995968 | bytes 7226041 | solution.py:142
  293.5 2.3 multiply_reduce_fusion.4
  304.8 1.8 constant_dynamic-update-slice_fusion.7
  306.5 2.6 fusion.156
  314.8 2.4 multiply_reduce_fusion.4
  326.2 1.8 constant_dynamic-update-slice_fusion.7
  328.0 2.6 fusion.156
  (122 shorter events, 34.8 us)
Async XLA Ops:
  7.2 113.3 %all-gather.11.cloned.1.call-start = ((), (), s32[]{:S(2)}) async-start(), calls=%async_computation.2 | async-start | bytes 2621440 | tf_op jit(solution)/shard_map/all_gather | solution.py:13
  7.2 37.1 %collective-permute-start = (bf16[2,1024,512]{2,1,0:T(8,128)(2,1)}, bf16[2,1024,512]{2,1,0:T(8,128)(2,1)}, u32[]{:S(2)}, u32[]{:S(2)}) collective-permute-start(bf16[2,1024,512]{2,1,0:T(8,128)(2,1)} %param.32), channel_id=1, source_target_pairs={{0,1},{1,2},{2,3},{3,4},{4,5},{5,6},{6,7},{7,8},{8,9},{9,10},{10,1... | collective-permute-start | bytes 6291464 | tf_op jit(solution)/shard_map/ppermute | solution.py:25
  9.1 39.7 %collective-permute-start.1 = (bf16[2,1024,512]{2,1,0:T(8,128)(2,1)}, bf16[2,1024,512]{2,1,0:T(8,128)(2,1)S(1)}, u32[]{:S(2)}, u32[]{:S(2)}) collective-permute-start(bf16[2,1024,512]{2,1,0:T(8,128)(2,1)} %param.32), channel_id=1, source_target_pairs={{1,0},{2,1},{3,2},{4,3},{5,4},{6,5},{7,6},{8,7},{9,8},{10,9},{11,1... | collective-permute-start | bytes 6291464 | tf_op jit(solution)/shard_map/ppermute | solution.py:27
  22.9 24.5 %copy-start.2 = (bf16[2,1024,512]{2,1,0:T(8,128)(2,1)S(1)}, bf16[2,1024,512]{2,1,0:T(8,128)(2,1)}, u32[]{:S(2)}) copy-start(bf16[2,1024,512]{2,1,0:T(8,128)(2,1)} %param.32) | copy-start | bytes 6291460
  48.8 1.6 copy-start.3
  50.4 10.6 %copy-start.1 = (bf16[4,256,256]{2,1,0:T(8,128)(2,1)S(1)}, bf16[4,256,256]{2,1,0:T(8,128)(2,1)}, u32[]{:S(2)}) copy-start(bf16[4,256,256]{2,1,0:T(8,128)(2,1)} %param.34) | copy-start | bytes 1572868
  50.4 19.6 %copy-start.9 = (s32[4]{0:T(128)S(1)}, s32[4]{0:T(128)}, u32[]{:S(2)}) copy-start(s32[4]{0:T(128)} %param.41) | copy-start | bytes 52
  50.4 20.0 %copy-start.8 = (s32[4,8]{1,0:T(4,128)S(1)}, s32[4,8]{1,0:T(4,128)}, u32[]{:S(2)}) copy-start(s32[4,8]{1,0:T(4,128)} %param.39) | copy-start | bytes 388
  52.1 152.6 %all-gather.9.cloned.1.call-start = ((), (), s32[]{:S(2)}) async-start(), calls=%async_computation.1 | async-start | bytes 2621440 | tf_op jit(solution)/shard_map/all_gather | solution.py:167
  52.2 29.2 %collective-permute-start.2 = (bf16[4,512,256]{2,1,0:T(8,128)(2,1)S(1)}, bf16[4,512,256]{2,1,0:T(8,128)(2,1)S(1)}, u32[]{:S(2)}, u32[]{:S(2)}) collective-permute-start(bf16[4,512,256]{2,1,0:T(8,128)(2,1)S(1)} %copy-done.3), channel_id=1, source_target_pairs={{0,1},{1,2},{2,3},{3,4},{4,5},{5,6},{6,7},{7,8},{8,9},{9,10},{10,1... | collective-permute-start | bytes 3145736 | tf_op jit(solution)/shard_map/ppermute | solution.py:25
  54.1 28.2 %collective-permute-start.3 = (bf16[4,512,256]{2,1,0:T(8,128)(2,1)S(1)}, bf16[4,512,256]{2,1,0:T(8,128)(2,1)}, u32[]{:S(2)}, u32[]{:S(2)}) collective-permute-start(bf16[4,512,256]{2,1,0:T(8,128)(2,1)S(1)} %copy-done.3), channel_id=1, source_target_pairs={{1,0},{2,1},{3,2},{4,3},{5,4},{6,5},{7,6},{8,7},{9,8},{10,9},{11,1... | collective-permute-start | bytes 3145736 | tf_op jit(solution)/shard_map/ppermute | solution.py:27
  61.1 16.1 %collective-permute-start.4 = (bf16[4,256,256]{2,1,0:T(8,128)(2,1)S(1)}, bf16[4,256,256]{2,1,0:T(8,128)(2,1)S(1)}, u32[]{:S(2)}, u32[]{:S(2)}) collective-permute-start(bf16[4,256,256]{2,1,0:T(8,128)(2,1)S(1)} %copy-done.1), channel_id=1, source_target_pairs={{0,1},{1,2},{2,3},{3,4},{4,5},{5,6},{6,7},{7,8},{8,9},{9,10},{10,1... | collective-permute-start | bytes 1572872 | tf_op jit(solution)/shard_map/ppermute | solution.py:25
  63.0 16.0 %collective-permute-start.5 = (bf16[4,256,256]{2,1,0:T(8,128)(2,1)S(1)}, bf16[4,256,256]{2,1,0:T(8,128)(2,1)}, u32[]{:S(2)}, u32[]{:S(2)}) collective-permute-start(bf16[4,256,256]{2,1,0:T(8,128)(2,1)S(1)} %copy-done.1), channel_id=1, source_target_pairs={{1,0},{2,1},{3,2},{4,3},{5,4},{6,5},{7,6},{8,7},{9,8},{10,9},{11,1... | collective-permute-start | bytes 1572872 | tf_op jit(solution)/shard_map/ppermute | solution.py:27
  81.3 1.0 copy-start.4
  104.3 18.7 %copy-start = (bf16[12,256,256]{2,1,0:T(8,128)(2,1)S(1)}, bf16[12,256,256]{2,1,0:T(8,128)(2,1)}, u32[]{:S(2)}) copy-start(bf16[12,256,256]{2,1,0:T(8,128)(2,1)} %pad_maximum_fusion.1) | copy-start | bytes 4718596
  104.3 18.7 %copy-start.5 = (s32[4,2]{0,1:T(2,128)S(1)}, s32[4,2]{0,1:T(2,128)}, u32[]{:S(2)}) copy-start(s32[4,2]{0,1:T(2,128)} %param.38) | copy-start | bytes 100
  104.3 18.7 %copy-start.6 = (f32[256]{0:T(256)S(1)}, f32[256]{0:T(256)}, u32[]{:S(2)}) copy-start(f32[256]{0:T(256)} %param.36) | copy-start | bytes 3076
  104.3 18.7 %copy-start.7 = (f32[4,256]{1,0:T(4,128)S(1)}, f32[4,256]{1,0:T(4,128)}, u32[]{:S(2)}) copy-start(f32[4,256]{1,0:T(4,128)} %param.35) | copy-start | bytes 12292
  104.3 18.7 %copy-start.10 = (f32[4,8]{1,0:T(4,128)S(1)}, f32[4,8]{1,0:T(4,128)}, u32[]{:S(2)}) copy-start(f32[4,8]{1,0:T(4,128)} %param.40) | copy-start | bytes 388
  104.3 18.7 %copy-start.11 = (s32[4]{0:T(128)S(1)}, s32[4]{0:T(128)}, u32[]{:S(2)}) copy-start(s32[4]{0:T(128)} %param.37) | copy-start | bytes 52
  166.0 73.1 %all-gather.7.cloned.1.call-start = ((), (), s32[]{:S(2)}) async-start(), calls=%async_computation | async-start | bytes 1310720 | tf_op jit(solution)/shard_map/all_gather | solution.py:166
  166.8 117.6 %all-gather.13.cloned.1.call-start = ((), (), s32[]{:S(2)}) async-start(), calls=%async_computation.3 | async-start | bytes 2621440 | tf_op jit(solution)/shard_map/all_gather | solution.py:13
  241.1 13.8 %collective-permute-start.6 = (bf16[4,256,256]{2,1,0:T(8,128)(2,1)S(1)}, bf16[4,256,256]{2,1,0:T(8,128)(2,1)S(1)}, u32[]{:S(2)}, u32[]{:S(2)}) collective-permute-start(bf16[4,256,256]{2,1,0:T(8,128)(2,1)S(1)} %broadcast_select_fusion.3), channel_id=1, source_target_pairs={{0,1},{1,2},{2,3},{3,4},{4,5},{5,6},{6,7},{7,8},{8,9},{9,10},{10,1... | collective-permute-start | bytes 1572872 | tf_op jit(solution)/shard_map/ppermute | solution.py:25
  243.0 13.6 %collective-permute-start.7 = (bf16[4,256,256]{2,1,0:T(8,128)(2,1)S(1)}, bf16[4,256,256]{2,1,0:T(8,128)(2,1)S(1)}, u32[]{:S(2)}, u32[]{:S(2)}) collective-permute-start(bf16[4,256,256]{2,1,0:T(8,128)(2,1)S(1)} %broadcast_select_fusion.3), channel_id=1, source_target_pairs={{1,0},{2,1},{3,2},{4,3},{5,4},{6,5},{7,6},{8,7},{9,8},{10,9},{11,1... | collective-permute-start | bytes 1572872 | tf_op jit(solution)/shard_map/ppermute | solution.py:27
Sparse Core Ops, SparseCore 0:
  52.2 68.1 all-gather.10
  166.2 38.5 all-gather.8
  207.4 31.6 all-gather.6
  241.7 42.6 all-gather.12
